TPU v7x, 32 devices: a whole 2x2x4 slice. The times are simulated.
32 devices in a mesh: groups: 2 (over x), freq: 16 (over z, y, core).
Axes of the slice: x: 2, y: 2, z: 4, core: 2. Of those that a mesh axis runs over, the one named last changes fastest.
Arguments:
- volts: bfloat16 [256, 68608], P(('groups', 'freq')), parts along dimension 0, may hold values from -6 to 6
- filter_taps: float32 [4, 1024], replicated, may hold values from -3 to 3
- kernel: float32 [63], replicated, may hold values from -0.5 to 0.5
Outputs:
- smoothed: bfloat16 [512, 256, 128], P(None, ('groups', 'freq')), parts along dimension 1
There are 2 independent parts, one for each index of `groups`. A program takes and returns all parts, laid end to end along the dimension named above; an argument that names none is the same for every part. Nothing has to cross between parts.
All inputs are finite; a program needn't handle non-finite values.
Results may differ from a plain program's by a relative error of at most 0.011.
Values may be sent and summed in bfloat16 or wider, within the bound.
A program may use at most 128 MiB of HBM per device.

v0:
```python
import jax
import jax.numpy as jnp
from jax import lax
from jax.sharding import PartitionSpec as P


def make_table(frame, channels):
    rows = jnp.arange(frame, dtype=jnp.int32)
    cols = jnp.arange(channels, dtype=jnp.int32)
    phase = (2 * rows[:, None] + 1 + channels) * (2 * cols[None, :] + 1) % (8 * channels)
    angle = phase.astype(jnp.float32) * (jnp.pi / (4.0 * channels))
    return (jnp.cos(angle) * (1.0 / jnp.sqrt(jnp.float32(channels)))).astype(jnp.bfloat16)


def make_band(weights, source_channel, channels):
    taps = weights.shape[0]
    half = (taps - 1) // 2
    target = jnp.arange(channels, dtype=jnp.int32)
    offset = source_channel[None, :] - target[:, None] + half

    def add_tap(step, band):
        return jnp.where(offset == step, weights[step], band)

    return lax.fori_loop(0, taps, add_tap, jnp.zeros((channels, channels), jnp.bfloat16))


def shards(volts, filter_taps, kernel):
    inp_dev, samples = volts.shape
    taps, frame = filter_taps.shape
    channels = frame // 2
    spectra = samples // frame - taps + 1
    groups_freq = lax.axis_size("freq")
    ch_dev = channels // groups_freq
    inputs = inp_dev * groups_freq
    blocks = volts.reshape(inp_dev, samples // frame, frame)
    filtered = jnp.zeros((inp_dev, spectra, frame), jnp.float32)
    for tap in range(taps):
        filtered = filtered + filter_taps[tap][None, None, :] * blocks[:, tap : tap + spectra, :]
    filtered = filtered.astype(jnp.bfloat16)
    table = make_table(frame, channels)
    chan = jnp.einsum("mc,ism->ics", table, filtered, preferred_element_type=jnp.float32)
    chan = chan.astype(jnp.bfloat16).reshape(inp_dev, groups_freq, ch_dev, spectra)
    scale = 1.0 / jnp.sqrt(jnp.float32(spectra))
    piece = lax.all_to_all(chan, "freq", split_axis=1, concat_axis=0, tiled=True)
    gram = jnp.einsum("iaks,jaks->kij", piece, piece, preferred_element_type=jnp.float32)
    vis = (gram * scale).astype(jnp.bfloat16)
    weights = kernel.astype(jnp.bfloat16)

    def send_plane(carry, plane):
        received = lax.all_to_all(
            plane.reshape(groups_freq, inp_dev, inputs),
            "freq",
            split_axis=0,
            concat_axis=0,
            tiled=True,
        )
        return (carry, received)

    unused, stacked = lax.scan(send_plane, jnp.zeros((), jnp.float32), vis)
    position = jnp.arange(channels, dtype=jnp.int32)
    source_channel = position % groups_freq * ch_dev + position // groups_freq
    band = make_band(weights, source_channel, channels)
    flat = stacked.reshape(channels, inp_dev * inputs)
    summed = jnp.dot(band, flat, preferred_element_type=jnp.float32)
    smoothed = summed.astype(jnp.bfloat16).reshape(channels, inp_dev, inputs)
    return smoothed


def solution(mesh):
    return jax.shard_map(
        shards,
        mesh=mesh,
        in_specs=(P(("groups", "freq"), None), P(), P()),
        out_specs=P(None, ("groups", "freq"), None),
        check_vma=False,
    )
```

profile of v0, /device:TPU:0, one launch (start us, length us, event | category | flops | bytes accessed | tf_op | source)
XLA Modules:
  0.0 494.1 jit_solution(8523371582949876706)
XLA Ops:
  3.1 12.7 %fusion.10 = bf16[8,512,64]{1,2,0:T(8,128)(2,1)S(1)} fusion(bf16[8,64,1024]{2,0,1:T(8,128)(2,1)S(1)} %get-tuple-element.138, bf16[8,64,1024]{2,0,1:T(8,128)(2,1)S(1)} %get-tuple-element.136, bf16[8,64,1024]{2,0,1:T(8,128)(2,1)S(1)} %get-tuple-element.137, bf16[8,64,1024]{2,0,1:T(8,128)(2,1)S(1)} %get-tuple-element.135, s32[512]{0:T(512)S(1)} %multiply_add_fusion.1, ...), kind=kOutput, calls=%fused_computation.21 | convolution fusion | flops 551813120 | bytes 4741120 | tf_op jit(solution)/shard_map/mc,ism->ics/dot_general | solution.py:41
  18.1 7.4 %all-to-all-start.1 = ((bf16[16,2,8192]{2,1,0:T(2,128)(2,1)}), bf16[16,2,8192]{2,1,0:T(2,128)(2,1)S(1)}, u32[]{:S(2)}, u32[]{:S(2)}) async-start(bf16[16,2,8192]{2,1,0:T(2,128)(2,1)} %reshape.68), calls=%async_computation.1 | async-start | bytes 1048576 | tf_op jit(solution)/shard_map/all_to_all | solution.py:44
  25.5 99.7 %while.25 = (s32[]{:T(128)}, bf16[512,512]{1,0:T(8,128)(2,1)S(1)}, bf16[63]{0:T(256)(128)(2,1)S(1)}, s32[512]{0:T(512)S(1)}, s32[]{:T(128)}, /*index=5*/s32[]{:T(128)}) while((s32[]{:T(128)}, bf16[512,512]{1,0:T(8,128)(2,1)S(1)}, bf16[63]{0:T(256)(128)(2,1)S(1)}, s32[512]{0:T(512)S(1)}, s32[]{:T(128)}, /*index=5*/s32[]{:T(128)}) %tuple.51), condition=%wide.region_1.2_spmd.clone, body=%wide.region_0.1_spmd.clone.sunk | while | flops 1310723 | bytes 1050717 | solution.py:24
  126.8 364.2 %while.24 = (s32[]{:T(128)}, bf16[32,16,8,128]{3,2,1,0:T(8,128)(2,1)}, bf16[32,128,128]{2,1,0:T(8,128)(2,1)S(1)}, s32[]{:T(128)}) while((s32[]{:T(128)}, bf16[32,16,8,128]{3,2,1,0:T(8,128)(2,1)}, bf16[32,128,128]{2,1,0:T(8,128)(2,1)S(1)}, s32[]{:T(128)}) %tuple.54), condition=%wide.region_3.4_spmd, body=%wide.region_2.3_spmd.sunk | while | flops 2 | bytes 229477 | solution.py:59
  133.4 6.6 %all-to-all-done = bf16[16,8,128]{2,1,0:T(8,128)(2,1)S(1)} async-done(((bf16[16,8,128]{2,1,0:T(8,128)(2,1)}), bf16[16,8,128]{2,1,0:T(8,128)(2,1)S(1)}, u32[]{:S(2)}, u32[]{:S(2)}) %all-to-all-start) | async-done | bytes 32800 | tf_op jit(solution)/shard_map/while/body/eval_jaxpr/all_to_all | solution.py:50
  144.7 6.6 %all-to-all-done = bf16[16,8,128]{2,1,0:T(8,128)(2,1)S(1)} async-done(((bf16[16,8,128]{2,1,0:T(8,128)(2,1)}), bf16[16,8,128]{2,1,0:T(8,128)(2,1)S(1)}, u32[]{:S(2)}, u32[]{:S(2)}) %all-to-all-start) | async-done | bytes 32800 | tf_op jit(solution)/shard_map/while/body/eval_jaxpr/all_to_all | solution.py:50
  156.0 6.6 %all-to-all-done = bf16[16,8,128]{2,1,0:T(8,128)(2,1)S(1)} async-done(((bf16[16,8,128]{2,1,0:T(8,128)(2,1)}), bf16[16,8,128]{2,1,0:T(8,128)(2,1)S(1)}, u32[]{:S(2)}, u32[]{:S(2)}) %all-to-all-start) | async-done | bytes 32800 | tf_op jit(solution)/shard_map/while/body/eval_jaxpr/all_to_all | solution.py:50
  167.3 6.6 %all-to-all-done = bf16[16,8,128]{2,1,0:T(8,128)(2,1)S(1)} async-done(((bf16[16,8,128]{2,1,0:T(8,128)(2,1)}), bf16[16,8,128]{2,1,0:T(8,128)(2,1)S(1)}, u32[]{:S(2)}, u32[]{:S(2)}) %all-to-all-start) | async-done | bytes 32800 | tf_op jit(solution)/shard_map/while/body/eval_jaxpr/all_to_all | solution.py:50
  178.6 6.6 %all-to-all-done = bf16[16,8,128]{2,1,0:T(8,128)(2,1)S(1)} async-done(((bf16[16,8,128]{2,1,0:T(8,128)(2,1)}), bf16[16,8,128]{2,1,0:T(8,128)(2,1)S(1)}, u32[]{:S(2)}, u32[]{:S(2)}) %all-to-all-start) | async-done | bytes 32800 | tf_op jit(solution)/shard_map/while/body/eval_jaxpr/all_to_all | solution.py:50
  189.9 6.6 %all-to-all-done = bf16[16,8,128]{2,1,0:T(8,128)(2,1)S(1)} async-done(((bf16[16,8,128]{2,1,0:T(8,128)(2,1)}), bf16[16,8,128]{2,1,0:T(8,128)(2,1)S(1)}, u32[]{:S(2)}, u32[]{:S(2)}) %all-to-all-start) | async-done | bytes 32800 | tf_op jit(solution)/shard_map/while/body/eval_jaxpr/all_to_all | solution.py:50
  201.2 6.6 %all-to-all-done = bf16[16,8,128]{2,1,0:T(8,128)(2,1)S(1)} async-done(((bf16[16,8,128]{2,1,0:T(8,128)(2,1)}), bf16[16,8,128]{2,1,0:T(8,128)(2,1)S(1)}, u32[]{:S(2)}, u32[]{:S(2)}) %all-to-all-start) | async-done | bytes 32800 | tf_op jit(solution)/shard_map/while/body/eval_jaxpr/all_to_all | solution.py:50
  212.5 6.6 %all-to-all-done = bf16[16,8,128]{2,1,0:T(8,128)(2,1)S(1)} async-done(((bf16[16,8,128]{2,1,0:T(8,128)(2,1)}), bf16[16,8,128]{2,1,0:T(8,128)(2,1)S(1)}, u32[]{:S(2)}, u32[]{:S(2)}) %all-to-all-start) | async-done | bytes 32800 | tf_op jit(solution)/shard_map/while/body/eval_jaxpr/all_to_all | solution.py:50
  223.8 6.6 %all-to-all-done = bf16[16,8,128]{2,1,0:T(8,128)(2,1)S(1)} async-done(((bf16[16,8,128]{2,1,0:T(8,128)(2,1)}), bf16[16,8,128]{2,1,0:T(8,128)(2,1)S(1)}, u32[]{:S(2)}, u32[]{:S(2)}) %all-to-all-start) | async-done | bytes 32800 | tf_op jit(solution)/shard_map/while/body/eval_jaxpr/all_to_all | solution.py:50
  235.1 6.6 %all-to-all-done = bf16[16,8,128]{2,1,0:T(8,128)(2,1)S(1)} async-done(((bf16[16,8,128]{2,1,0:T(8,128)(2,1)}), bf16[16,8,128]{2,1,0:T(8,128)(2,1)S(1)}, u32[]{:S(2)}, u32[]{:S(2)}) %all-to-all-start) | async-done | bytes 32800 | tf_op jit(solution)/shard_map/while/body/eval_jaxpr/all_to_all | solution.py:50
  246.4 6.6 %all-to-all-done = bf16[16,8,128]{2,1,0:T(8,128)(2,1)S(1)} async-done(((bf16[16,8,128]{2,1,0:T(8,128)(2,1)}), bf16[16,8,128]{2,1,0:T(8,128)(2,1)S(1)}, u32[]{:S(2)}, u32[]{:S(2)}) %all-to-all-start) | async-done | bytes 32800 | tf_op jit(solution)/shard_map/while/body/eval_jaxpr/all_to_all | solution.py:50
  257.7 6.6 %all-to-all-done = bf16[16,8,128]{2,1,0:T(8,128)(2,1)S(1)} async-done(((bf16[16,8,128]{2,1,0:T(8,128)(2,1)}), bf16[16,8,128]{2,1,0:T(8,128)(2,1)S(1)}, u32[]{:S(2)}, u32[]{:S(2)}) %all-to-all-start) | async-done | bytes 32800 | tf_op jit(solution)/shard_map/while/body/eval_jaxpr/all_to_all | solution.py:50
  269.0 6.6 %all-to-all-done = bf16[16,8,128]{2,1,0:T(8,128)(2,1)S(1)} async-done(((bf16[16,8,128]{2,1,0:T(8,128)(2,1)}), bf16[16,8,128]{2,1,0:T(8,128)(2,1)S(1)}, u32[]{:S(2)}, u32[]{:S(2)}) %all-to-all-start) | async-done | bytes 32800 | tf_op jit(solution)/shard_map/while/body/eval_jaxpr/all_to_all | solution.py:50
  280.3 6.6 %all-to-all-done = bf16[16,8,128]{2,1,0:T(8,128)(2,1)S(1)} async-done(((bf16[16,8,128]{2,1,0:T(8,128)(2,1)}), bf16[16,8,128]{2,1,0:T(8,128)(2,1)S(1)}, u32[]{:S(2)}, u32[]{:S(2)}) %all-to-all-start) | async-done | bytes 32800 | tf_op jit(solution)/shard_map/while/body/eval_jaxpr/all_to_all | solution.py:50
  291.6 6.6 %all-to-all-done = bf16[16,8,128]{2,1,0:T(8,128)(2,1)S(1)} async-done(((bf16[16,8,128]{2,1,0:T(8,128)(2,1)}), bf16[16,8,128]{2,1,0:T(8,128)(2,1)S(1)}, u32[]{:S(2)}, u32[]{:S(2)}) %all-to-all-start) | async-done | bytes 32800 | tf_op jit(solution)/shard_map/while/body/eval_jaxpr/all_to_all | solution.py:50
  302.9 6.6 %all-to-all-done = bf16[16,8,128]{2,1,0:T(8,128)(2,1)S(1)} async-done(((bf16[16,8,128]{2,1,0:T(8,128)(2,1)}), bf16[16,8,128]{2,1,0:T(8,128)(2,1)S(1)}, u32[]{:S(2)}, u32[]{:S(2)}) %all-to-all-start) | async-done | bytes 32800 | tf_op jit(solution)/shard_map/while/body/eval_jaxpr/all_to_all | solution.py:50
  314.2 6.6 %all-to-all-done = bf16[16,8,128]{2,1,0:T(8,128)(2,1)S(1)} async-done(((bf16[16,8,128]{2,1,0:T(8,128)(2,1)}), bf16[16,8,128]{2,1,0:T(8,128)(2,1)S(1)}, u32[]{:S(2)}, u32[]{:S(2)}) %all-to-all-start) | async-done | bytes 32800 | tf_op jit(solution)/shard_map/while/body/eval_jaxpr/all_to_all | solution.py:50
  359.4 6.6 %all-to-all-done = bf16[16,8,128]{2,1,0:T(8,128)(2,1)S(1)} async-done(((bf16[16,8,128]{2,1,0:T(8,128)(2,1)}), bf16[16,8,128]{2,1,0:T(8,128)(2,1)S(1)}, u32[]{:S(2)}, u32[]{:S(2)}) %all-to-all-start) | async-done | bytes 32800 | tf_op jit(solution)/shard_map/while/body/eval_jaxpr/all_to_all | solution.py:50
  393.3 6.6 %all-to-all-done = bf16[16,8,128]{2,1,0:T(8,128)(2,1)S(1)} async-done(((bf16[16,8,128]{2,1,0:T(8,128)(2,1)}), bf16[16,8,128]{2,1,0:T(8,128)(2,1)S(1)}, u32[]{:S(2)}, u32[]{:S(2)}) %all-to-all-start) | async-done | bytes 32800 | tf_op jit(solution)/shard_map/while/body/eval_jaxpr/all_to_all | solution.py:50
  427.2 6.6 %all-to-all-done = bf16[16,8,128]{2,1,0:T(8,128)(2,1)S(1)} async-done(((bf16[16,8,128]{2,1,0:T(8,128)(2,1)}), bf16[16,8,128]{2,1,0:T(8,128)(2,1)S(1)}, u32[]{:S(2)}, u32[]{:S(2)}) %all-to-all-start) | async-done | bytes 32800 | tf_op jit(solution)/shard_map/while/body/eval_jaxpr/all_to_all | solution.py:50
  (254 shorter events, 340.5 us)
Async XLA Ops:
  18.1 107.2 %all-to-all-start.1 = ((bf16[16,2,8192]{2,1,0:T(2,128)(2,1)}), bf16[16,2,8192]{2,1,0:T(2,128)(2,1)S(1)}, u32[]{:S(2)}, u32[]{:S(2)}) async-start(bf16[16,2,8192]{2,1,0:T(2,128)(2,1)} %reshape.68), calls=%async_computation.1 | async-start | bytes 1048576 | tf_op jit(solution)/shard_map/all_to_all | solution.py:44
  127.4 12.6 %all-to-all-start = ((bf16[16,8,128]{2,1,0:T(8,128)(2,1)}), bf16[16,8,128]{2,1,0:T(8,128)(2,1)S(1)}, u32[]{:S(2)}, u32[]{:S(2)}) async-start(bf16[16,8,128]{2,1,0:T(8,128)(2,1)} %dynamic-slice_bitcast_fusion.2), calls=%async_computation | async-start | bytes 65536 | tf_op jit(solution)/shard_map/while/body/eval_jaxpr/all_to_all | solution.py:50
  141.3 10.1 %all-to-all-start = ((bf16[16,8,128]{2,1,0:T(8,128)(2,1)}), bf16[16,8,128]{2,1,0:T(8,128)(2,1)S(1)}, u32[]{:S(2)}, u32[]{:S(2)}) async-start(bf16[16,8,128]{2,1,0:T(8,128)(2,1)} %dynamic-slice_bitcast_fusion.2), calls=%async_computation | async-start | bytes 65536 | tf_op jit(solution)/shard_map/while/body/eval_jaxpr/all_to_all | solution.py:50
  152.6 10.1 %all-to-all-start = ((bf16[16,8,128]{2,1,0:T(8,128)(2,1)}), bf16[16,8,128]{2,1,0:T(8,128)(2,1)S(1)}, u32[]{:S(2)}, u32[]{:S(2)}) async-start(bf16[16,8,128]{2,1,0:T(8,128)(2,1)} %dynamic-slice_bitcast_fusion.2), calls=%async_computation | async-start | bytes 65536 | tf_op jit(solution)/shard_map/while/body/eval_jaxpr/all_to_all | solution.py:50
  163.9 10.1 %all-to-all-start = ((bf16[16,8,128]{2,1,0:T(8,128)(2,1)}), bf16[16,8,128]{2,1,0:T(8,128)(2,1)S(1)}, u32[]{:S(2)}, u32[]{:S(2)}) async-start(bf16[16,8,128]{2,1,0:T(8,128)(2,1)} %dynamic-slice_bitcast_fusion.2), calls=%async_computation | async-start | bytes 65536 | tf_op jit(solution)/shard_map/while/body/eval_jaxpr/all_to_all | solution.py:50
  175.2 10.1 %all-to-all-start = ((bf16[16,8,128]{2,1,0:T(8,128)(2,1)}), bf16[16,8,128]{2,1,0:T(8,128)(2,1)S(1)}, u32[]{:S(2)}, u32[]{:S(2)}) async-start(bf16[16,8,128]{2,1,0:T(8,128)(2,1)} %dynamic-slice_bitcast_fusion.2), calls=%async_computation | async-start | bytes 65536 | tf_op jit(solution)/shard_map/while/body/eval_jaxpr/all_to_all | solution.py:50
  186.5 10.1 %all-to-all-start = ((bf16[16,8,128]{2,1,0:T(8,128)(2,1)}), bf16[16,8,128]{2,1,0:T(8,128)(2,1)S(1)}, u32[]{:S(2)}, u32[]{:S(2)}) async-start(bf16[16,8,128]{2,1,0:T(8,128)(2,1)} %dynamic-slice_bitcast_fusion.2), calls=%async_computation | async-start | bytes 65536 | tf_op jit(solution)/shard_map/while/body/eval_jaxpr/all_to_all | solution.py:50
  197.8 10.1 %all-to-all-start = ((bf16[16,8,128]{2,1,0:T(8,128)(2,1)}), bf16[16,8,128]{2,1,0:T(8,128)(2,1)S(1)}, u32[]{:S(2)}, u32[]{:S(2)}) async-start(bf16[16,8,128]{2,1,0:T(8,128)(2,1)} %dynamic-slice_bitcast_fusion.2), calls=%async_computation | async-start | bytes 65536 | tf_op jit(solution)/shard_map/while/body/eval_jaxpr/all_to_all | solution.py:50
  209.1 10.1 %all-to-all-start = ((bf16[16,8,128]{2,1,0:T(8,128)(2,1)}), bf16[16,8,128]{2,1,0:T(8,128)(2,1)S(1)}, u32[]{:S(2)}, u32[]{:S(2)}) async-start(bf16[16,8,128]{2,1,0:T(8,128)(2,1)} %dynamic-slice_bitcast_fusion.2), calls=%async_computation | async-start | bytes 65536 | tf_op jit(solution)/shard_map/while/body/eval_jaxpr/all_to_all | solution.py:50
  220.4 10.1 %all-to-all-start = ((bf16[16,8,128]{2,1,0:T(8,128)(2,1)}), bf16[16,8,128]{2,1,0:T(8,128)(2,1)S(1)}, u32[]{:S(2)}, u32[]{:S(2)}) async-start(bf16[16,8,128]{2,1,0:T(8,128)(2,1)} %dynamic-slice_bitcast_fusion.2), calls=%async_computation | async-start | bytes 65536 | tf_op jit(solution)/shard_map/while/body/eval_jaxpr/all_to_all | solution.py:50
  231.7 10.1 %all-to-all-start = ((bf16[16,8,128]{2,1,0:T(8,128)(2,1)}), bf16[16,8,128]{2,1,0:T(8,128)(2,1)S(1)}, u32[]{:S(2)}, u32[]{:S(2)}) async-start(bf16[16,8,128]{2,1,0:T(8,128)(2,1)} %dynamic-slice_bitcast_fusion.2), calls=%async_computation | async-start | bytes 65536 | tf_op jit(solution)/shard_map/while/body/eval_jaxpr/all_to_all | solution.py:50
  243.0 10.1 %all-to-all-start = ((bf16[16,8,128]{2,1,0:T(8,128)(2,1)}), bf16[16,8,128]{2,1,0:T(8,128)(2,1)S(1)}, u32[]{:S(2)}, u32[]{:S(2)}) async-start(bf16[16,8,128]{2,1,0:T(8,128)(2,1)} %dynamic-slice_bitcast_fusion.2), calls=%async_computation | async-start | bytes 65536 | tf_op jit(solution)/shard_map/while/body/eval_jaxpr/all_to_all | solution.py:50
  254.3 10.1 %all-to-all-start = ((bf16[16,8,128]{2,1,0:T(8,128)(2,1)}), bf16[16,8,128]{2,1,0:T(8,128)(2,1)S(1)}, u32[]{:S(2)}, u32[]{:S(2)}) async-start(bf16[16,8,128]{2,1,0:T(8,128)(2,1)} %dynamic-slice_bitcast_fusion.2), calls=%async_computation | async-start | bytes 65536 | tf_op jit(solution)/shard_map/while/body/eval_jaxpr/all_to_all | solution.py:50
  265.6 10.1 %all-to-all-start = ((bf16[16,8,128]{2,1,0:T(8,128)(2,1)}), bf16[16,8,128]{2,1,0:T(8,128)(2,1)S(1)}, u32[]{:S(2)}, u32[]{:S(2)}) async-start(bf16[16,8,128]{2,1,0:T(8,128)(2,1)} %dynamic-slice_bitcast_fusion.2), calls=%async_computation | async-start | bytes 65536 | tf_op jit(solution)/shard_map/while/body/eval_jaxpr/all_to_all | solution.py:50
  276.9 10.1 %all-to-all-start = ((bf16[16,8,128]{2,1,0:T(8,128)(2,1)}), bf16[16,8,128]{2,1,0:T(8,128)(2,1)S(1)}, u32[]{:S(2)}, u32[]{:S(2)}) async-start(bf16[16,8,128]{2,1,0:T(8,128)(2,1)} %dynamic-slice_bitcast_fusion.2), calls=%async_computation | async-start | bytes 65536 | tf_op jit(solution)/shard_map/while/body/eval_jaxpr/all_to_all | solution.py:50
  288.2 10.1 %all-to-all-start = ((bf16[16,8,128]{2,1,0:T(8,128)(2,1)}), bf16[16,8,128]{2,1,0:T(8,128)(2,1)S(1)}, u32[]{:S(2)}, u32[]{:S(2)}) async-start(bf16[16,8,128]{2,1,0:T(8,128)(2,1)} %dynamic-slice_bitcast_fusion.2), calls=%async_computation | async-start | bytes 65536 | tf_op jit(solution)/shard_map/while/body/eval_jaxpr/all_to_all | solution.py:50
  299.5 10.1 %all-to-all-start = ((bf16[16,8,128]{2,1,0:T(8,128)(2,1)}), bf16[16,8,128]{2,1,0:T(8,128)(2,1)S(1)}, u32[]{:S(2)}, u32[]{:S(2)}) async-start(bf16[16,8,128]{2,1,0:T(8,128)(2,1)} %dynamic-slice_bitcast_fusion.2), calls=%async_computation | async-start | bytes 65536 | tf_op jit(solution)/shard_map/while/body/eval_jaxpr/all_to_all | solution.py:50
  310.8 10.1 %all-to-all-start = ((bf16[16,8,128]{2,1,0:T(8,128)(2,1)}), bf16[16,8,128]{2,1,0:T(8,128)(2,1)S(1)}, u32[]{:S(2)}, u32[]{:S(2)}) async-start(bf16[16,8,128]{2,1,0:T(8,128)(2,1)} %dynamic-slice_bitcast_fusion.2), calls=%async_computation | async-start | bytes 65536 | tf_op jit(solution)/shard_map/while/body/eval_jaxpr/all_to_all | solution.py:50
  322.1 10.1 %all-to-all-start = ((bf16[16,8,128]{2,1,0:T(8,128)(2,1)}), bf16[16,8,128]{2,1,0:T(8,128)(2,1)S(1)}, u32[]{:S(2)}, u32[]{:S(2)}) async-start(bf16[16,8,128]{2,1,0:T(8,128)(2,1)} %dynamic-slice_bitcast_fusion.2), calls=%async_computation | async-start | bytes 65536 | tf_op jit(solution)/shard_map/while/body/eval_jaxpr/all_to_all | solution.py:50
  333.4 10.1 %all-to-all-start = ((bf16[16,8,128]{2,1,0:T(8,128)(2,1)}), bf16[16,8,128]{2,1,0:T(8,128)(2,1)S(1)}, u32[]{:S(2)}, u32[]{:S(2)}) async-start(bf16[16,8,128]{2,1,0:T(8,128)(2,1)} %dynamic-slice_bitcast_fusion.2), calls=%async_computation | async-start | bytes 65536 | tf_op jit(solution)/shard_map/while/body/eval_jaxpr/all_to_all | solution.py:50
  344.7 10.1 %all-to-all-start = ((bf16[16,8,128]{2,1,0:T(8,128)(2,1)}), bf16[16,8,128]{2,1,0:T(8,128)(2,1)S(1)}, u32[]{:S(2)}, u32[]{:S(2)}) async-start(bf16[16,8,128]{2,1,0:T(8,128)(2,1)} %dynamic-slice_bitcast_fusion.2), calls=%async_computation | async-start | bytes 65536 | tf_op jit(solution)/shard_map/while/body/eval_jaxpr/all_to_all | solution.py:50
  356.0 10.1 %all-to-all-start = ((bf16[16,8,128]{2,1,0:T(8,128)(2,1)}), bf16[16,8,128]{2,1,0:T(8,128)(2,1)S(1)}, u32[]{:S(2)}, u32[]{:S(2)}) async-start(bf16[16,8,128]{2,1,0:T(8,128)(2,1)} %dynamic-slice_bitcast_fusion.2), calls=%async_computation | async-start | bytes 65536 | tf_op jit(solution)/shard_map/while/body/eval_jaxpr/all_to_all | solution.py:50
  367.3 10.1 %all-to-all-start = ((bf16[16,8,128]{2,1,0:T(8,128)(2,1)}), bf16[16,8,128]{2,1,0:T(8,128)(2,1)S(1)}, u32[]{:S(2)}, u32[]{:S(2)}) async-start(bf16[16,8,128]{2,1,0:T(8,128)(2,1)} %dynamic-slice_bitcast_fusion.2), calls=%async_computation | async-start | bytes 65536 | tf_op jit(solution)/shard_map/while/body/eval_jaxpr/all_to_all | solution.py:50
  378.6 10.1 %all-to-all-start = ((bf16[16,8,128]{2,1,0:T(8,128)(2,1)}), bf16[16,8,128]{2,1,0:T(8,128)(2,1)S(1)}, u32[]{:S(2)}, u32[]{:S(2)}) async-start(bf16[16,8,128]{2,1,0:T(8,128)(2,1)} %dynamic-slice_bitcast_fusion.2), calls=%async_computation | async-start | bytes 65536 | tf_op jit(solution)/shard_map/while/body/eval_jaxpr/all_to_all | solution.py:50
  (11 other events, 95.3 us)
where the time goes:
time: 499 us; the launch traced here: 494 us
  waiting for transfers between devices  211 us (42%)
  starting transfers between devices  121 us (24%)
  local copies, waits for them, and re-layouts  83.9 us (17%)
  other arithmetic  61.1 us (12%)
  matrix products  15.5 us (3%)
    all_to_all x32, waiting for transfers between devices, send_plane(): lax.all_to_all(plane.reshape(groups_freq, inp_dev, inputs), 'freq', split...  211 us
    all_to_all x32, starting transfers between devices, send_plane(): lax.all_to_all(plane.reshape(groups_freq, inp_dev, inputs), 'freq', split...  113 us
    select_n x63, other arithmetic, add_tap(): return jnp.where(offset == step, weights[step], band)  61.1 us
    dynamic_slice x63, local copies, waits for them, and re-layouts, add_tap(): return jnp.where(offset == step, weights[step], band)  37.5 us
    dynamic_update_slice x32, local copies, waits for them, and re-layouts, shards(): unused, stacked = lax.scan(send_plane, jnp.zeros((), jnp.float32), vis)  19.7 us
    reshape x32, local copies, waits for them, and re-layouts, send_plane(): plane.reshape(groups_freq, inp_dev, inputs)  19.6 us
    dot_general x1, matrix products, shards(): jnp.einsum('mc,ism->ics', table, filtered, preferred_element_type=jnp.flo...  12.7 us
  transfers between devices with their start and end apart: 33, of which 32 were waited for; matrix products, arithmetic and copies ran while one was open for 20% of the time, Pallas kernels for 0%

commit v1 on v0

v1 whole, which is shorter than its diff:
```python
import functools

import jax
import jax.numpy as jnp
import ml_dtypes
import numpy as np
from jax import lax
from jax.experimental import pallas as pl
from jax.experimental.pallas import tpu as pltpu
from jax.sharding import PartitionSpec as P

NT = (((1,), (1,)), ((), ()))


def make_table(frame, channels, devices):
    order = np.arange(channels).reshape(devices, channels // devices // 2, 2)
    order = order.transpose(2, 0, 1).reshape(-1)
    rows = np.arange(frame)
    phase = (2 * rows[None, :] + 1 + channels) * (2 * order[:, None] + 1) % (8 * channels)
    angle = phase.astype(np.float32) * np.float32(np.pi / (4.0 * channels))
    scale = np.float32(1.0) / np.sqrt(np.float32(channels))
    return (np.cos(angle) * scale).astype(ml_dtypes.bfloat16)


def correlate(
    n, chunks, volts, taps, kernel, table, out,
    frames, framesb, product, chan_f, chan_send, chan_recv, vis_send, vis_recv, rows_f, planes, window,
    send1, recv1, send2, recv2,
):
    groups = lax.axis_index("groups")
    me = lax.axis_index("freq")
    ntaps, frame = taps.shape
    channels = table.shape[0]
    inp, samples = volts.shape
    spectra = samples // frame - ntaps + 1
    pairs = channels // n // 2
    step = pairs // chunks
    inputs = n * inp
    half = channels // 2

    barrier = pltpu.get_barrier_semaphore()

    def greet(p, _):
        pl.semaphore_signal(
            barrier, inc=1, device_id=(groups, lax.rem(me + p, n)),
            device_id_type=pl.DeviceIdType.MESH,
        )
        return 0

    lax.fori_loop(1, n, greet, 0)

    def filter_lanes(mb, _):
        base = pl.multiple_of(mb * 128, 128)
        weights = [jnp.broadcast_to(taps[t : t + 1, pl.ds(base, 128)], (inp, 128)) for t in range(ntaps)]

        def block(s):
            at = pl.multiple_of(s * frame + base, 128)
            return volts[:, pl.ds(at, 128)].astype(jnp.float32)

        held = [block(s) for s in range(ntaps - 1)]
        for s in range(spectra):
            held.append(block(s + ntaps - 1))
            total = weights[0] * held[0]
            for t in range(1, ntaps):
                total = total + weights[t] * held[t]
            frames.at[mb][pl.ds(s, inp, stride=spectra), :] = total
            held = held[1:]
        return 0

    lax.fori_loop(0, frame // 128, filter_lanes, 0)
    for mb in range(frame // 128):
        framesb[:, mb * 128 : (mb + 1) * 128] = frames[mb].astype(jnp.bfloat16)

    product[...] = lax.dot_general(table[...], framesb[...], NT, preferred_element_type=jnp.float32)
    low = lax.broadcasted_iota(jnp.int32, (half, 128), 1) < spectra
    for p in range(inp // 2):
        even = product[:half, 128 * p : 128 * (p + 1)]
        odd = product[half:, 128 * p : 128 * (p + 1)]
        chan_f[pl.ds(2 * p, half, stride=inp), :] = jnp.where(low, even, pltpu.roll(odd, spectra, 1))
        chan_f[pl.ds(2 * p + 1, half, stride=inp), :] = jnp.where(low, pltpu.roll(even, spectra, 1), odd)
    chan_send[...] = chan_f[...].reshape(n, pairs, inp, 128).astype(jnp.bfloat16)

    def copy1(c, peer, source):
        at = pl.ds(c * step, step)
        return pltpu.make_async_remote_copy(
            src_ref=chan_send.at[peer, at], dst_ref=chan_recv.at[source, at],
            send_sem=send1.at[c, peer], recv_sem=recv1.at[c, source],
            device_id=(groups, peer), device_id_type=pl.DeviceIdType.MESH,
        )

    def copy2(c, peer, source):
        at = pl.ds(2 * c * step, 2 * step)
        return pltpu.make_async_remote_copy(
            src_ref=vis_send.at[peer, at], dst_ref=vis_recv.at[source, at],
            send_sem=send2.at[c, peer], recv_sem=recv2.at[c, source],
            device_id=(groups, peer), device_id_type=pl.DeviceIdType.MESH,
        )

    def each_peer(act):
        def body(p, _):
            act(lax.rem(me + p, n))
            return 0

        lax.fori_loop(1, n, body, 0)

    pl.semaphore_wait(barrier, n - 1)
    for c in range(chunks):
        each_peer(lambda peer: copy1(c, peer, me).start())
    chan_recv[me] = chan_send[me]

    count = kernel.shape[1]
    reach = (count - 1) // 2
    window[...] = jnp.zeros_like(window)
    window[0:1, 0:count] = kernel[...].astype(jnp.bfloat16).astype(jnp.float32)
    spread = jnp.broadcast_to(window[0:1, :], (128, 256))
    band = pltpu.roll(spread, 64 - reach, 1, stride=1, stride_axis=0).astype(jnp.bfloat16)

    scale = 1.0 / (spectra**0.5)
    lane = lax.broadcasted_iota(jnp.int32, (inputs, 128), 1)
    for c in range(chunks):
        each_peer(lambda peer: copy1(c, peer, peer).wait_recv())

        def gram(k, _):
            both = chan_recv[:, k].astype(jnp.float32).reshape(inputs, 128)
            right = both.astype(jnp.bfloat16)
            for parity in range(2):
                left = jnp.where((lane < spectra) == (parity == 0), both, 0.0).astype(jnp.bfloat16)
                vis = lax.dot_general(left, right, NT, preferred_element_type=jnp.float32) * scale
                vis_send[:, 2 * k + parity] = vis.reshape(n, inp, inputs).astype(jnp.bfloat16)
            return 0

        lax.fori_loop(c * step, (c + 1) * step, gram, 0)
        each_peer(lambda peer: copy2(c, peer, me).start())
    vis_recv[me] = vis_send[me]
    for c in range(chunks):
        each_peer(lambda peer: copy2(c, peer, peer).wait_recv())

    planes[0:64, :] = jnp.zeros((64, inp * 128), jnp.bfloat16)
    planes[64 + channels :, :] = jnp.zeros((64, inp * 128), jnp.bfloat16)

    def smooth(j, _):
        lanes = pl.ds(pl.multiple_of(j * 128, 128), 128)
        rows_f[...] = vis_recv[:, :, :, lanes].astype(jnp.float32).reshape(channels * inp, 128)
        for i in range(inp):
            planes[64 : 64 + channels, i * 128 : (i + 1) * 128] = (
                rows_f[pl.ds(i, channels, stride=inp), :].astype(jnp.bfloat16)
            )
        for r in range(channels // 128):
            done = jnp.dot(band, planes[r * 128 : r * 128 + 256, :], preferred_element_type=jnp.float32)
            for i in range(inp):
                rows_f[pl.ds(r * 128 * inp + i, 128, stride=inp), :] = done[:, i * 128 : (i + 1) * 128]
        out[:, :, lanes] = rows_f[...].reshape(channels, inp, 128).astype(jnp.bfloat16)
        return 0

    lax.fori_loop(0, inputs // 128, smooth, 0)
    for c in range(chunks):
        each_peer(lambda peer: copy1(c, peer, me).wait_send())
        each_peer(lambda peer: copy2(c, peer, me).wait_send())


def shards(volts, filter_taps, kernel):
    inp, samples = volts.shape
    ntaps, frame = filter_taps.shape
    channels = frame // 2
    spectra = samples // frame - ntaps + 1
    n = lax.axis_size("freq")
    ch_dev = channels // n
    pairs = ch_dev // 2
    inputs = n * inp
    chunks = min(4, pairs)
    table = jnp.asarray(make_table(frame, channels, n))
    vmem = pl.BlockSpec(memory_space=pltpu.VMEM)
    bf16, f32 = jnp.bfloat16, jnp.float32
    return pl.pallas_call(
        functools.partial(correlate, n, chunks),
        out_shape=jax.ShapeDtypeStruct((channels, inp, inputs), bf16),
        in_specs=[vmem] * 4,
        out_specs=vmem,
        scratch_shapes=[
            pltpu.VMEM((frame // 128, inp * spectra, 128), f32),
            pltpu.VMEM((inp * spectra, frame), bf16),
            pltpu.VMEM((channels, inp * spectra), f32),
            pltpu.VMEM((channels // 2 * inp, 128), f32),
            pltpu.VMEM((n, pairs, inp, 128), bf16),
            pltpu.VMEM((n, pairs, inp, 128), bf16),
            pltpu.VMEM((n, ch_dev, inp, inputs), bf16),
            pltpu.VMEM((n, ch_dev, inp, inputs), bf16),
            pltpu.VMEM((channels * inp, 128), f32),
            pltpu.VMEM((channels + 128, inp * 128), bf16),
            pltpu.VMEM((8, 256), f32),
            pltpu.SemaphoreType.DMA((chunks, n)),
            pltpu.SemaphoreType.DMA((chunks, n)),
            pltpu.SemaphoreType.DMA((chunks, n)),
            pltpu.SemaphoreType.DMA((chunks, n)),
        ],
        compiler_params=pltpu.CompilerParams(
            collective_id=0, has_side_effects=True, vmem_limit_bytes=56 << 20
        ),
        name="correlate",
    )(volts, filter_taps, kernel.reshape(1, -1), table)


def solution(mesh):
    return jax.shard_map(
        shards,
        mesh=mesh,
        in_specs=(P(("groups", "freq"), None), P(), P()),
        out_specs=P(None, ("groups", "freq"), None),
        check_vma=False,
    )
```

time: 499 us -> 50.2 us (0.10)
  waiting for transfers between devices: 211 us -> 0 us
  starting transfers between devices: 121 us -> 0 us
  local copies, waits for them, and re-layouts: 83.9 us -> 2.26 us
  other arithmetic: 61.1 us -> 0 us
  Pallas kernels: 0 us -> 47.7 us
  matrix products: 15.5 us -> 0 us
    all_to_all x33 -> x0, waiting for transfers between devices: 211 us -> none  [the longest x32 211 us: send_plane(): lax.all_to_all(plane.reshape(groups_freq, inp_dev, inputs), 'freq', split...]
    all_to_all x33 -> x0, starting transfers between devices: 121 us -> none  [the longest x32 113 us: send_plane(): lax.all_to_all(plane.reshape(groups_freq, inp_dev, inputs), 'freq', split...]
    select_n x63 -> x0, other arithmetic: 61.1 us -> none  [add_tap(): return jnp.where(offset == step, weights[step], band)]
    pallas_call x0 -> x1, Pallas kernels: none -> 47.7 us  [shards(): pl.pallas_call(functools.partial(correlate, n, chunks), out_shape=jax.Sha...]
    dynamic_slice x63 -> x0, local copies, waits for them, and re-layouts: 37.5 us -> none  [add_tap(): return jnp.where(offset == step, weights[step], band)]
    dynamic_update_slice x32 -> x0, local copies, waits for them, and re-layouts: 19.7 us -> none  [shards(): unused, stacked = lax.scan(send_plane, jnp.zeros((), jnp.float32), vis)]
    reshape x33 -> x0, local copies, waits for them, and re-layouts: 19.7 us -> none  [the longest x32 19.6 us: send_plane(): plane.reshape(groups_freq, inp_dev, inputs)]
    dot_general x3 -> x0, matrix products: 15.5 us -> none  [the longest x1 12.7 us: shards(): jnp.einsum('mc,ism->ics', table, filtered, preferred_element_type=jnp.flo...]
  transfers between devices with their start and end apart: 33 -> 0, of which waited for: 32 -> 0; matrix products, arithmetic and copies ran while one was open for 20% -> 0% of each run, Pallas kernels for 0% -> 0%
where the time goes in v1:
time: 50.2 us; the launch traced here: 50 us
  Pallas kernels  47.7 us (95%)
  local copies, waits for them, and re-layouts  2.26 us (5%)
    pallas_call x1, Pallas kernels, shards(): pl.pallas_call(functools.partial(correlate, n, chunks), out_shape=jax.Sha...  47.7 us
    unnamed x1, local copies, waits for them, and re-layouts  2.26 us

profile of v1, /device:TPU:0, one launch (start us, length us, event | category | flops | bytes accessed | tf_op | source)
XLA Modules:
  0.0 50.0 jit_solution(5897898908472521092)
XLA Ops:
  0.0 47.7 %correlate.1 = bf16[512,8,128]{2,1,0:T(8,128)(2,1)} custom-call(bf16[8,68608]{1,0:T(8,128)(2,1)} %volts.1, f32[4,1024]{1,0:T(4,128)} %taps.1, f32[1,63]{1,0:T(1,128)} %bitcast.1, bf16[512,1024]{1,0:T(8,128)(2,1)} %constant.2.clone.table), custom_call_target="tpu_custom_call" | custom-call | tf_op jit(solution)/shard_map/correlate/pallas_call | solution.py:174
  47.7 2.3 %copy.6 = bf16[512,8,128]{2,1,0:T(8,128)(2,1)} copy(bf16[512,8,128]{2,1,0:T(8,128)(2,1)} %correlate.1) | data formatting | bytes 2097152

commit v2 on v1

--- a/solution.py
+++ b/solution.py
@@ -24,11 +24,15 @@
 
 def correlate(
     n, chunks, volts, taps, kernel, table, out,
-    frames, framesb, product, chan_f, chan_send, chan_recv, vis_send, vis_recv, rows_f, planes, window,
-    send1, recv1, send2, recv2,
+    frames, framesb, product, chan_f, chan_send, chan_recv, chan_half,
+    vis_send, half_send, cross_send, vis, packed, rows_f, planes, window,
+    sent, got_chan, got_half, got_vis, got_packed,
 ):
     groups = lax.axis_index("groups")
     me = lax.axis_index("freq")
+    m = n // 2
+    side = lax.div(me, m)
+    place = lax.rem(me, m)
     ntaps, frame = taps.shape
     channels = table.shape[0]
     inp, samples = volts.shape
@@ -80,33 +84,62 @@
         chan_f[pl.ds(2 * p + 1, half, stride=inp), :] = jnp.where(low, pltpu.roll(even, spectra, 1), odd)
     chan_send[...] = chan_f[...].reshape(n, pairs, inp, 128).astype(jnp.bfloat16)
 
-    def copy1(c, peer, source):
-        at = pl.ds(c * step, step)
+    def remote(src, dst, send_sem, recv_sem, peer):
         return pltpu.make_async_remote_copy(
-            src_ref=chan_send.at[peer, at], dst_ref=chan_recv.at[source, at],
-            send_sem=send1.at[c, peer], recv_sem=recv1.at[c, source],
+            src_ref=src, dst_ref=dst, send_sem=send_sem, recv_sem=recv_sem,
             device_id=(groups, peer), device_id_type=pl.DeviceIdType.MESH,
         )
 
-    def copy2(c, peer, source):
-        at = pl.ds(2 * c * step, 2 * step)
-        return pltpu.make_async_remote_copy(
-            src_ref=vis_send.at[peer, at], dst_ref=vis_recv.at[source, at],
-            send_sem=send2.at[c, peer], recv_sem=recv2.at[c, source],
-            device_id=(groups, peer), device_id_type=pl.DeviceIdType.MESH,
-        )
-
-    def each_peer(act):
+    def full_chan(c, peer, source):
+        at = pl.ds(c * step, step)
+        owner = 2 * lax.rem(peer, m) + lax.div(peer, m)
+        return remote(
+            chan_send.at[owner, at], chan_recv.at[source, at],
+            sent.at[0, c, peer], got_chan.at[c, source], peer,
+        )
+
+    def half_chan(c, spot, source):
+        at = pl.ds(c * step, step)
+        return remote(
+            chan_send.at[2 * spot + 1 - side, at], chan_half.at[source, at],
+            sent.at[1, c, spot], got_half.at[c, source], side * m + spot,
+        )
+
+    def full_vis(c, spot, source):
+        at = pl.ds(c * step, step)
+        return remote(
+            vis_send.at[spot, at], vis.at[source, side, at],
+            sent.at[2, c, spot], got_vis.at[c, source], side * m + spot,
+        )
+
+    def half_vis(c, spot, source):
+        at = pl.ds(c * step, step)
+        return remote(
+            half_send.at[spot, at], packed.at[side, source, at],
+            sent.at[3, c, spot], got_packed.at[0, c, source], side * m + spot,
+        )
+
+    def cross_vis(c, spot, source, column_side):
+        at = pl.ds(c * step, step)
+        return remote(
+            cross_send.at[spot, at], packed.at[column_side, source, at],
+            sent.at[4, c, spot], got_packed.at[1, c, source], (1 - side) * m + spot,
+        )
+
+    def loop(first, act):
         def body(p, _):
-            act(lax.rem(me + p, n))
+            act(lax.rem(place + p, m))
             return 0
 
-        lax.fori_loop(1, n, body, 0)
+        lax.fori_loop(first, m, body, 0)
 
     pl.semaphore_wait(barrier, n - 1)
     for c in range(chunks):
-        each_peer(lambda peer: copy1(c, peer, me).start())
-    chan_recv[me] = chan_send[me]
+        loop(0, lambda spot: full_chan(c, (1 - side) * m + spot, me).start())
+        loop(1, lambda spot: full_chan(c, side * m + spot, me).start())
+        loop(1, lambda spot: half_chan(c, spot, place).start())
+    chan_recv[me] = chan_send[2 * place + side]
+    chan_half[place] = chan_send[2 * place + 1 - side]
 
     count = kernel.shape[1]
     reach = (count - 1) // 2
@@ -116,31 +149,67 @@
     band = pltpu.roll(spread, 64 - reach, 1, stride=1, stride_axis=0).astype(jnp.bfloat16)
 
     scale = 1.0 / (spectra**0.5)
-    lane = lax.broadcasted_iota(jnp.int32, (inputs, 128), 1)
-    for c in range(chunks):
-        each_peer(lambda peer: copy1(c, peer, peer).wait_recv())
+    ours = inputs // 2
+    first = lax.broadcasted_iota(jnp.int32, (ours, 128), 1) < spectra
+    lower = lax.broadcasted_iota(jnp.int32, (pairs, inp, inputs), 2) < ours
+
+    def rows_of(value):
+        return value.astype(jnp.float32).reshape(-1, 128)
+
+    def product_of(left, right):
+        return lax.dot_general(left, right, NT, preferred_element_type=jnp.float32) * scale
+
+    def parities(value):
+        return [
+            jnp.where(first, value, 0.0).astype(jnp.bfloat16),
+            jnp.where(first, 0.0, value).astype(jnp.bfloat16),
+        ]
+
+    for c in range(chunks):
+        loop(0, lambda spot: full_chan(c, me, (1 - side) * m + spot).wait_recv())
+        loop(1, lambda spot: full_chan(c, me, side * m + spot).wait_recv())
+        loop(1, lambda spot: half_chan(c, place, spot).wait_recv())
 
         def gram(k, _):
-            both = chan_recv[:, k].astype(jnp.float32).reshape(inputs, 128)
-            right = both.astype(jnp.bfloat16)
+            every = rows_of(chan_recv[:, k]).astype(jnp.bfloat16)
+            own = parities(rows_of(chan_recv[pl.ds(side * m, m), k]))
+            other = rows_of(chan_recv[pl.ds((1 - side) * m, m), k]).astype(jnp.bfloat16)
+            cross = product_of(other, jnp.concatenate(own, axis=0))
+            cross_send[:, k] = cross.reshape(m, inp, inputs).astype(jnp.bfloat16)
             for parity in range(2):
-                left = jnp.where((lane < spectra) == (parity == 0), both, 0.0).astype(jnp.bfloat16)
-                vis = lax.dot_general(left, right, NT, preferred_element_type=jnp.float32) * scale
-                vis_send[:, 2 * k + parity] = vis.reshape(n, inp, inputs).astype(jnp.bfloat16)
+                full = product_of(own[parity], every)
+                vis_send[:, k, parity] = full.reshape(m, inp, inputs).astype(jnp.bfloat16)
+            mine = rows_of(chan_half[:, k])
+            within = product_of(mine.astype(jnp.bfloat16), jnp.concatenate(parities(mine), axis=0))
+            half_send[:, k] = within.reshape(m, inp, inputs).astype(jnp.bfloat16)
             return 0
 
         lax.fori_loop(c * step, (c + 1) * step, gram, 0)
-        each_peer(lambda peer: copy2(c, peer, me).start())
-    vis_recv[me] = vis_send[me]
-    for c in range(chunks):
-        each_peer(lambda peer: copy2(c, peer, peer).wait_recv())
+        loop(0, lambda spot: cross_vis(c, spot, place, side).start())
+        loop(1, lambda spot: full_vis(c, spot, place).start())
+        loop(1, lambda spot: half_vis(c, spot, place).start())
+    vis[place, side] = vis_send[place]
+    packed[side, place] = half_send[place]
+    for c in range(chunks):
+        loop(0, lambda spot: cross_vis(c, place, spot, 1 - side).wait_recv())
+        loop(1, lambda spot: full_vis(c, place, spot).wait_recv())
+        loop(1, lambda spot: half_vis(c, place, spot).wait_recv())
+
+    def unpack(spot, _):
+        left = packed[0, spot].astype(jnp.float32)
+        right = packed[1, spot].astype(jnp.float32)
+        vis[spot, 1 - side, :, 0] = jnp.where(lower, left, pltpu.roll(right, ours, 2)).astype(jnp.bfloat16)
+        vis[spot, 1 - side, :, 1] = jnp.where(lower, pltpu.roll(left, ours, 2), right).astype(jnp.bfloat16)
+        return 0
+
+    lax.fori_loop(0, m, unpack, 0)
 
     planes[0:64, :] = jnp.zeros((64, inp * 128), jnp.bfloat16)
     planes[64 + channels :, :] = jnp.zeros((64, inp * 128), jnp.bfloat16)
 
     def smooth(j, _):
         lanes = pl.ds(pl.multiple_of(j * 128, 128), 128)
-        rows_f[...] = vis_recv[:, :, :, lanes].astype(jnp.float32).reshape(channels * inp, 128)
+        rows_f[...] = vis[:, :, :, :, :, lanes].astype(jnp.float32).reshape(channels * inp, 128)
         for i in range(inp):
             planes[64 : 64 + channels, i * 128 : (i + 1) * 128] = (
                 rows_f[pl.ds(i, channels, stride=inp), :].astype(jnp.bfloat16)
@@ -154,8 +223,12 @@
 
     lax.fori_loop(0, inputs // 128, smooth, 0)
     for c in range(chunks):
-        each_peer(lambda peer: copy1(c, peer, me).wait_send())
-        each_peer(lambda peer: copy2(c, peer, me).wait_send())
+        loop(0, lambda spot: full_chan(c, (1 - side) * m + spot, me).wait_send())
+        loop(1, lambda spot: full_chan(c, side * m + spot, me).wait_send())
+        loop(1, lambda spot: half_chan(c, spot, place).wait_send())
+        loop(0, lambda spot: cross_vis(c, spot, place, side).wait_send())
+        loop(1, lambda spot: full_vis(c, spot, place).wait_send())
+        loop(1, lambda spot: half_vis(c, spot, place).wait_send())
 
 
 def shards(volts, filter_taps, kernel):
@@ -183,15 +256,20 @@
             pltpu.VMEM((channels // 2 * inp, 128), f32),
             pltpu.VMEM((n, pairs, inp, 128), bf16),
             pltpu.VMEM((n, pairs, inp, 128), bf16),
-            pltpu.VMEM((n, ch_dev, inp, inputs), bf16),
-            pltpu.VMEM((n, ch_dev, inp, inputs), bf16),
+            pltpu.VMEM((n // 2, pairs, inp, 128), bf16),
+            pltpu.VMEM((n // 2, pairs, 2, inp, inputs), bf16),
+            pltpu.VMEM((n // 2, pairs, inp, inputs), bf16),
+            pltpu.VMEM((n // 2, pairs, inp, inputs), bf16),
+            pltpu.VMEM((n // 2, 2, pairs, 2, inp, inputs), bf16),
+            pltpu.VMEM((2, n // 2, pairs, inp, inputs), bf16),
             pltpu.VMEM((channels * inp, 128), f32),
             pltpu.VMEM((channels + 128, inp * 128), bf16),
             pltpu.VMEM((8, 256), f32),
+            pltpu.SemaphoreType.DMA((5, chunks, n)),
             pltpu.SemaphoreType.DMA((chunks, n)),
-            pltpu.SemaphoreType.DMA((chunks, n)),
-            pltpu.SemaphoreType.DMA((chunks, n)),
-            pltpu.SemaphoreType.DMA((chunks, n)),
+            pltpu.SemaphoreType.DMA((chunks, n // 2)),
+            pltpu.SemaphoreType.DMA((chunks, n // 2)),
+            pltpu.SemaphoreType.DMA((2, chunks, n // 2)),
         ],
         compiler_params=pltpu.CompilerParams(
             collective_id=0, has_side_effects=True, vmem_limit_bytes=56 << 20

time: 50.2 us -> 45.8 us (0.912)
  Pallas kernels: 47.7 us -> 43.4 us
    pallas_call x1, Pallas kernels: 47.7 us -> 43.4 us  [shards(): pl.pallas_call(functools.partial(correlate, n, chunks), out_shape=jax.Sha...]
where the time goes in v2:
time: 45.8 us; the launch traced here: 45.6 us
  Pallas kernels  43.4 us (95%)
  local copies, waits for them, and re-layouts  2.26 us (5%)
    pallas_call x1, Pallas kernels, shards(): pl.pallas_call(functools.partial(correlate, n, chunks), out_shape=jax.Sha...  43.4 us
    unnamed x1, local copies, waits for them, and re-layouts  2.26 us

profile of v2, /device:TPU:0, one launch (start us, length us, event | category | flops | bytes accessed | tf_op | source)
XLA Modules:
  0.0 45.6 jit_solution(2005377862758900326)
XLA Ops:
  0.0 43.4 %correlate.1 = bf16[512,8,128]{2,1,0:T(8,128)(2,1)} custom-call(bf16[8,68608]{1,0:T(8,128)(2,1)} %volts.1, f32[4,1024]{1,0:T(4,128)} %taps.1, f32[1,63]{1,0:T(1,128)} %bitcast.1, bf16[512,1024]{1,0:T(8,128)(2,1)} %constant.2.clone.table), custom_call_target="tpu_custom_call" | custom-call | tf_op jit(solution)/shard_map/correlate/pallas_call | solution.py:247
  43.4 2.3 %copy.6 = bf16[512,8,128]{2,1,0:T(8,128)(2,1)} copy(bf16[512,8,128]{2,1,0:T(8,128)(2,1)} %correlate.1) | data formatting | bytes 2097152

commit v3 on v2

--- a/solution.py
+++ b/solution.py
@@ -23,10 +23,11 @@
 
 
 def correlate(
-    n, chunks, volts, taps, kernel, table, out,
+    n, chunks, volts_hbm, taps, kernel, table_hbm, out,
+    volts, table,
     frames, framesb, product, chan_f, chan_send, chan_recv, chan_half,
     vis_send, half_send, cross_send, vis, packed, rows_f, planes, window,
-    sent, got_chan, got_half, got_vis, got_packed,
+    sent, got, fetched,
 ):
     groups = lax.axis_index("groups")
     me = lax.axis_index("freq")
@@ -53,6 +54,14 @@
 
     lax.fori_loop(1, n, greet, 0)
 
+    fetch = [
+        pltpu.make_async_copy(volts_hbm, volts, fetched.at[0]),
+        pltpu.make_async_copy(table_hbm, table, fetched.at[1]),
+    ]
+    for copy in fetch:
+        copy.start()
+    fetch[0].wait()
+
     def filter_lanes(mb, _):
         base = pl.multiple_of(mb * 128, 128)
         weights = [jnp.broadcast_to(taps[t : t + 1, pl.ds(base, 128)], (inp, 128)) for t in range(ntaps)]
@@ -75,6 +84,7 @@
     for mb in range(frame // 128):
         framesb[:, mb * 128 : (mb + 1) * 128] = frames[mb].astype(jnp.bfloat16)
 
+    fetch[1].wait()
     product[...] = lax.dot_general(table[...], framesb[...], NT, preferred_element_type=jnp.float32)
     low = lax.broadcasted_iota(jnp.int32, (half, 128), 1) < spectra
     for p in range(inp // 2):
@@ -90,40 +100,46 @@
             device_id=(groups, peer), device_id_type=pl.DeviceIdType.MESH,
         )
 
+    def arrived(whole, kind, c):
+        remote(whole, whole, sent.at[kind], got.at[kind, c], (1 - side) * m + place).wait_recv()
+
+    def departed(whole, kind):
+        remote(whole, whole, sent.at[kind], got.at[kind, 0], (1 - side) * m + place).wait_send()
+
     def full_chan(c, peer, source):
         at = pl.ds(c * step, step)
         owner = 2 * lax.rem(peer, m) + lax.div(peer, m)
         return remote(
             chan_send.at[owner, at], chan_recv.at[source, at],
-            sent.at[0, c, peer], got_chan.at[c, source], peer,
+            sent.at[0], got.at[0, c], peer,
         )
 
     def half_chan(c, spot, source):
         at = pl.ds(c * step, step)
         return remote(
             chan_send.at[2 * spot + 1 - side, at], chan_half.at[source, at],
-            sent.at[1, c, spot], got_half.at[c, source], side * m + spot,
+            sent.at[1], got.at[1, c], side * m + spot,
         )
 
     def full_vis(c, spot, source):
         at = pl.ds(c * step, step)
         return remote(
             vis_send.at[spot, at], vis.at[source, side, at],
-            sent.at[2, c, spot], got_vis.at[c, source], side * m + spot,
+            sent.at[2], got.at[2, c], side * m + spot,
         )
 
     def half_vis(c, spot, source):
         at = pl.ds(c * step, step)
         return remote(
             half_send.at[spot, at], packed.at[side, source, at],
-            sent.at[3, c, spot], got_packed.at[0, c, source], side * m + spot,
+            sent.at[3], got.at[3, c], side * m + spot,
         )
 
     def cross_vis(c, spot, source, column_side):
         at = pl.ds(c * step, step)
         return remote(
             cross_send.at[spot, at], packed.at[column_side, source, at],
-            sent.at[4, c, spot], got_packed.at[1, c, source], (1 - side) * m + spot,
+            sent.at[4], got.at[4, c], (1 - side) * m + spot,
         )
 
     def loop(first, act):
@@ -166,9 +182,9 @@
         ]
 
     for c in range(chunks):
-        loop(0, lambda spot: full_chan(c, me, (1 - side) * m + spot).wait_recv())
-        loop(1, lambda spot: full_chan(c, me, side * m + spot).wait_recv())
-        loop(1, lambda spot: half_chan(c, place, spot).wait_recv())
+        at = pl.ds(c * step, step)
+        arrived(chan_recv.at[pl.ds(0, n - 1), at], 0, c)
+        arrived(chan_half.at[pl.ds(0, m - 1), at], 1, c)
 
         def gram(k, _):
             every = rows_of(chan_recv[:, k]).astype(jnp.bfloat16)
@@ -191,9 +207,10 @@
     vis[place, side] = vis_send[place]
     packed[side, place] = half_send[place]
     for c in range(chunks):
-        loop(0, lambda spot: cross_vis(c, place, spot, 1 - side).wait_recv())
-        loop(1, lambda spot: full_vis(c, place, spot).wait_recv())
-        loop(1, lambda spot: half_vis(c, place, spot).wait_recv())
+        at = pl.ds(c * step, step)
+        arrived(vis.at[pl.ds(0, m - 1), side, at], 2, c)
+        arrived(packed.at[side, pl.ds(0, m - 1), at], 3, c)
+        arrived(packed.at[1 - side, pl.ds(0, m), at], 4, c)
 
     def unpack(spot, _):
         left = packed[0, spot].astype(jnp.float32)
@@ -222,13 +239,11 @@
         return 0
 
     lax.fori_loop(0, inputs // 128, smooth, 0)
-    for c in range(chunks):
-        loop(0, lambda spot: full_chan(c, (1 - side) * m + spot, me).wait_send())
-        loop(1, lambda spot: full_chan(c, side * m + spot, me).wait_send())
-        loop(1, lambda spot: half_chan(c, spot, place).wait_send())
-        loop(0, lambda spot: cross_vis(c, spot, place, side).wait_send())
-        loop(1, lambda spot: full_vis(c, spot, place).wait_send())
-        loop(1, lambda spot: half_vis(c, spot, place).wait_send())
+    departed(chan_send.at[pl.ds(0, n - 1)], 0)
+    departed(chan_send.at[pl.ds(0, m - 1)], 1)
+    departed(vis_send.at[pl.ds(0, m - 1)], 2)
+    departed(half_send.at[pl.ds(0, m - 1)], 3)
+    departed(cross_send.at[pl.ds(0, m)], 4)
 
 
 def shards(volts, filter_taps, kernel):
@@ -240,16 +255,19 @@
     ch_dev = channels // n
     pairs = ch_dev // 2
     inputs = n * inp
-    chunks = min(4, pairs)
+    chunks = min(2, pairs)
     table = jnp.asarray(make_table(frame, channels, n))
     vmem = pl.BlockSpec(memory_space=pltpu.VMEM)
+    hbm = pl.BlockSpec(memory_space=pl.ANY)
     bf16, f32 = jnp.bfloat16, jnp.float32
     return pl.pallas_call(
         functools.partial(correlate, n, chunks),
         out_shape=jax.ShapeDtypeStruct((channels, inp, inputs), bf16),
-        in_specs=[vmem] * 4,
+        in_specs=[hbm, vmem, vmem, hbm],
         out_specs=vmem,
         scratch_shapes=[
+            pltpu.VMEM(volts.shape, bf16),
+            pltpu.VMEM(table.shape, bf16),
             pltpu.VMEM((frame // 128, inp * spectra, 128), f32),
             pltpu.VMEM((inp * spectra, frame), bf16),
             pltpu.VMEM((channels, inp * spectra), f32),
@@ -265,11 +283,9 @@
             pltpu.VMEM((channels * inp, 128), f32),
             pltpu.VMEM((channels + 128, inp * 128), bf16),
             pltpu.VMEM((8, 256), f32),
-            pltpu.SemaphoreType.DMA((5, chunks, n)),
-            pltpu.SemaphoreType.DMA((chunks, n)),
-            pltpu.SemaphoreType.DMA((chunks, n // 2)),
-            pltpu.SemaphoreType.DMA((chunks, n // 2)),
-            pltpu.SemaphoreType.DMA((2, chunks, n // 2)),
+            pltpu.SemaphoreType.DMA((5,)),
+            pltpu.SemaphoreType.DMA((5, chunks)),
+            pltpu.SemaphoreType.DMA((2,)),
         ],
         compiler_params=pltpu.CompilerParams(
             collective_id=0, has_side_effects=True, vmem_limit_bytes=56 << 20

time: 45.8 us -> 39.6 us (0.86)
  Pallas kernels: 43.4 us -> 37 us
    pallas_call x1, Pallas kernels: 43.4 us -> 37 us  [shards(): pl.pallas_call(functools.partial(correlate, n, chunks), out_shape=jax.Sha...]
where the time goes in v3:
time: 39.6 us; the launch traced here: 39.3 us
  Pallas kernels  37 us (93%)
  local copies, waits for them, and re-layouts  2.26 us (6%)
    pallas_call x1, Pallas kernels, shards(): pl.pallas_call(functools.partial(correlate, n, chunks), out_shape=jax.Sha...  37 us
    unnamed x1, local copies, waits for them, and re-layouts  2.26 us

profile of v3, /device:TPU:0, one launch (start us, length us, event | category | flops | bytes accessed | tf_op | source)
XLA Modules:
  0.0 39.3 jit_solution(7104477793280222994)
XLA Ops:
  0.0 37.0 %correlate.1 = bf16[512,8,128]{2,1,0:T(8,128)(2,1)} custom-call(bf16[8,68608]{1,0:T(8,128)(2,1)} %volts_hbm.1, f32[4,1024]{1,0:T(4,128)} %taps.1, f32[1,63]{1,0:T(1,128)} %bitcast.1, bf16[512,1024]{1,0:T(8,128)(2,1)} %constant.2.clone.table_hbm), custom_call_target="tpu_custom_call" | custom-call | tf_op jit(solution)/shard_map/correlate/pallas_call | solution.py:263
  37.1 2.3 %copy.6 = bf16[512,8,128]{2,1,0:T(8,128)(2,1)} copy(bf16[512,8,128]{2,1,0:T(8,128)(2,1)} %correlate.1) | data formatting | bytes 2097152

commit v4 on v3

--- a/solution.py
+++ b/solution.py
@@ -23,11 +23,11 @@
 
 
 def correlate(
-    n, chunks, volts_hbm, taps, kernel, table_hbm, out,
+    n, chunks, volts_hbm, taps, kernel, table_hbm, out_hbm,
     volts, table,
     frames, framesb, product, chan_f, chan_send, chan_recv, chan_half,
-    vis_send, half_send, cross_send, vis, packed, rows_f, planes, window,
-    sent, got, fetched,
+    vis_send, half_send, cross_send, vis, packed, rows_f, planes, window, out,
+    sent, got, fetched, stored,
 ):
     groups = lax.axis_index("groups")
     me = lax.axis_index("freq")
@@ -167,7 +167,7 @@
     scale = 1.0 / (spectra**0.5)
     ours = inputs // 2
     first = lax.broadcasted_iota(jnp.int32, (ours, 128), 1) < spectra
-    lower = lax.broadcasted_iota(jnp.int32, (pairs, inp, inputs), 2) < ours
+    lower = lax.broadcasted_iota(jnp.int32, (step, inp, inputs), 2) < ours
 
     def rows_of(value):
         return value.astype(jnp.float32).reshape(-1, 128)
@@ -212,14 +212,16 @@
         arrived(packed.at[side, pl.ds(0, m - 1), at], 3, c)
         arrived(packed.at[1 - side, pl.ds(0, m), at], 4, c)
 
-    def unpack(spot, _):
-        left = packed[0, spot].astype(jnp.float32)
-        right = packed[1, spot].astype(jnp.float32)
-        vis[spot, 1 - side, :, 0] = jnp.where(lower, left, pltpu.roll(right, ours, 2)).astype(jnp.bfloat16)
-        vis[spot, 1 - side, :, 1] = jnp.where(lower, pltpu.roll(left, ours, 2), right).astype(jnp.bfloat16)
-        return 0
-
-    lax.fori_loop(0, m, unpack, 0)
+        def unpack(spot, _):
+            left = packed[0, spot, at].astype(jnp.float32)
+            right = packed[1, spot, at].astype(jnp.float32)
+            even = jnp.where(lower, left, pltpu.roll(right, ours, 2))
+            odd = jnp.where(lower, pltpu.roll(left, ours, 2), right)
+            vis[spot, 1 - side, at, 0] = even.astype(jnp.bfloat16)
+            vis[spot, 1 - side, at, 1] = odd.astype(jnp.bfloat16)
+            return 0
+
+        lax.fori_loop(0, m, unpack, 0)
 
     planes[0:64, :] = jnp.zeros((64, inp * 128), jnp.bfloat16)
     planes[64 + channels :, :] = jnp.zeros((64, inp * 128), jnp.bfloat16)
@@ -235,7 +237,13 @@
             done = jnp.dot(band, planes[r * 128 : r * 128 + 256, :], preferred_element_type=jnp.float32)
             for i in range(inp):
                 rows_f[pl.ds(r * 128 * inp + i, 128, stride=inp), :] = done[:, i * 128 : (i + 1) * 128]
-        out[:, :, lanes] = rows_f[...].reshape(channels, inp, 128).astype(jnp.bfloat16)
+            rows = rows_f[r * 128 * inp : (r + 1) * 128 * inp, :]
+            out[r * 128 : (r + 1) * 128, :, lanes] = rows.reshape(128, inp, 128).astype(jnp.bfloat16)
+            pltpu.make_async_copy(
+                out.at[r * 128 : (r + 1) * 128, :, lanes],
+                out_hbm.at[r * 128 : (r + 1) * 128, :, lanes],
+                stored.at[0],
+            ).start()
         return 0
 
     lax.fori_loop(0, inputs // 128, smooth, 0)
@@ -244,6 +252,7 @@
     departed(vis_send.at[pl.ds(0, m - 1)], 2)
     departed(half_send.at[pl.ds(0, m - 1)], 3)
     departed(cross_send.at[pl.ds(0, m)], 4)
+    pltpu.make_async_copy(out, out_hbm, stored.at[0]).wait()
 
 
 def shards(volts, filter_taps, kernel):
@@ -264,7 +273,7 @@
         functools.partial(correlate, n, chunks),
         out_shape=jax.ShapeDtypeStruct((channels, inp, inputs), bf16),
         in_specs=[hbm, vmem, vmem, hbm],
-        out_specs=vmem,
+        out_specs=hbm,
         scratch_shapes=[
             pltpu.VMEM(volts.shape, bf16),
             pltpu.VMEM(table.shape, bf16),
@@ -283,9 +292,11 @@
             pltpu.VMEM((channels * inp, 128), f32),
             pltpu.VMEM((channels + 128, inp * 128), bf16),
             pltpu.VMEM((8, 256), f32),
+            pltpu.VMEM((channels, inp, inputs), bf16),
             pltpu.SemaphoreType.DMA((5,)),
             pltpu.SemaphoreType.DMA((5, chunks)),
             pltpu.SemaphoreType.DMA((2,)),
+            pltpu.SemaphoreType.DMA((1,)),
         ],
         compiler_params=pltpu.CompilerParams(
             collective_id=0, has_side_effects=True, vmem_limit_bytes=56 << 20

time: 39.6 us -> 39.2 us (0.990)
  no operation moved by 1% of the time
where the time goes in v4:
time: 39.2 us; the launch traced here: 39 us
  Pallas kernels  36.7 us (94%)
  local copies, waits for them, and re-layouts  2.26 us (6%)
    pallas_call x1, Pallas kernels, shards(): pl.pallas_call(functools.partial(correlate, n, chunks), out_shape=jax.Sha...  36.7 us
    unnamed x1, local copies, waits for them, and re-layouts  2.26 us

profile of v4, /device:TPU:0, one launch (start us, length us, event | category | flops | bytes accessed | tf_op | source)
XLA Modules:
  0.0 39.0 jit_solution(11687923147311417465)
XLA Ops:
  0.0 36.7 %correlate.1 = bf16[512,8,128]{2,1,0:T(8,128)(2,1)} custom-call(bf16[8,68608]{1,0:T(8,128)(2,1)} %volts_hbm.1, f32[4,1024]{1,0:T(4,128)} %taps.1, f32[1,63]{1,0:T(1,128)} %bitcast.1, bf16[512,1024]{1,0:T(8,128)(2,1)} %constant.2.clone.table_hbm), custom_call_target="tpu_custom_call" | custom-call | tf_op jit(solution)/shard_map/correlate/pallas_call | solution.py:272
  36.7 2.3 %copy.6 = bf16[512,8,128]{2,1,0:T(8,128)(2,1)} copy(bf16[512,8,128]{2,1,0:T(8,128)(2,1)} %correlate.1) | data formatting | bytes 2097152

commit v5 on v4

--- a/solution.py
+++ b/solution.py
@@ -164,6 +164,9 @@
     spread = jnp.broadcast_to(window[0:1, :], (128, 256))
     band = pltpu.roll(spread, 64 - reach, 1, stride=1, stride_axis=0).astype(jnp.bfloat16)
 
+    planes[0:64, :] = jnp.zeros((64, inp * 128), jnp.bfloat16)
+    planes[64 + channels :, :] = jnp.zeros((64, inp * 128), jnp.bfloat16)
+
     scale = 1.0 / (spectra**0.5)
     ours = inputs // 2
     first = lax.broadcasted_iota(jnp.int32, (ours, 128), 1) < spectra
@@ -223,8 +226,6 @@
 
         lax.fori_loop(0, m, unpack, 0)
 
-    planes[0:64, :] = jnp.zeros((64, inp * 128), jnp.bfloat16)
-    planes[64 + channels :, :] = jnp.zeros((64, inp * 128), jnp.bfloat16)
 
     def smooth(j, _):
         lanes = pl.ds(pl.multiple_of(j * 128, 128), 128)

time: 39.2 us -> 39.2 us (level)
  no operation moved by 1% of the time
where the time goes in v5:
time: 39.2 us; the launch traced here: 39 us
  Pallas kernels  36.7 us (94%)
  local copies, waits for them, and re-layouts  2.26 us (6%)
    pallas_call x1, Pallas kernels, shards(): pl.pallas_call(functools.partial(correlate, n, chunks), out_shape=jax.Sha...  36.7 us
    unnamed x1, local copies, waits for them, and re-layouts  2.26 us

profile of v5, /device:TPU:0, one launch (start us, length us, event | category | flops | bytes accessed | tf_op | source)
XLA Modules:
  0.0 39.0 jit_solution(9696843555375249843)
XLA Ops:
  0.0 36.7 %correlate.1 = bf16[512,8,128]{2,1,0:T(8,128)(2,1)} custom-call(bf16[8,68608]{1,0:T(8,128)(2,1)} %volts_hbm.1, f32[4,1024]{1,0:T(4,128)} %taps.1, f32[1,63]{1,0:T(1,128)} %bitcast.1, bf16[512,1024]{1,0:T(8,128)(2,1)} %constant.2.clone.table_hbm), custom_call_target="tpu_custom_call" | custom-call | tf_op jit(solution)/shard_map/correlate/pallas_call | solution.py:273
  36.7 2.3 %copy.6 = bf16[512,8,128]{2,1,0:T(8,128)(2,1)} copy(bf16[512,8,128]{2,1,0:T(8,128)(2,1)} %correlate.1) | data formatting | bytes 2097152
